TPU v7x, 256 devices: a whole 4x4x8 slice. The times are simulated.
256 devices in a mesh: gx: 32 (over y, z), gy: 8 (over x, core).
Axes of the slice: x: 4, y: 4, z: 8, core: 2. Of those that a mesh axis runs over, the one named last changes fastest.
Arguments:
- densities: bfloat16 [24576, 32, 128], P(('gx', 'gy')), may hold values from -6 to 6
- geometry: float32 [24576, 7, 128], P(('gx', 'gy')), as said below
- near_ids: int32 [24576, 8], P(('gx', 'gy')), may hold values from 0 to 24575, as said below
- basis_in: bfloat16 [24576, 64, 128], P(('gx', 'gy')), may hold values from -0.5 to 0.5
- basis_out: bfloat16 [24576, 64, 128], P(('gx', 'gy')), may hold values from -0.75 to 0.75
- leaf_up: bfloat16 [24576, 64, 64], P(('gx', 'gy')), may hold values from -0.078125 to 0.078125
- leaf_down: bfloat16 [24576, 64, 64], P(('gx', 'gy')), may hold values from -0.75 to 0.75
- leaf_coupling: bfloat16 [24576, 6, 64, 64], P(('gx', 'gy')), may hold values from -0.3125 to 0.3125
- leaf_far: int32 [24576, 6], P(('gx', 'gy')), may hold values from 0 to 24575, as said below
- leaf_count: int32 [24576], P(('gx', 'gy')), may hold values from 1 to 6, as said below
- cluster_up: bfloat16 [256, 64, 64], P(('gx', 'gy')), may hold values from -0.25 to 0.25
- cluster_down: bfloat16 [256, 64, 64], P(('gx', 'gy')), may hold values from -0.75 to 0.75
- cluster_coupling: bfloat16 [256, 6, 64, 64], P(('gx', 'gy')), may hold values from -0.3125 to 0.3125
- cluster_far: int32 [256, 6], P(('gx', 'gy')), may hold values from 0 to 255, as said below
- group_up: bfloat16 [32, 64, 64], replicated, may hold values from -0.375 to 0.375
- group_down: bfloat16 [32, 64, 64], P('gx'), may hold values from -0.75 to 0.75
- group_coupling: bfloat16 [32, 6, 64, 64], P('gx'), may hold values from -0.3125 to 0.3125
- group_far: int32 [32, 6], P('gx'), may hold values from 0 to 31, as said below
- root_coupling: bfloat16 [8, 8, 64, 64], replicated, may hold values from -0.25 to 0.25
Outputs:
- potential: float32 [24576, 32, 128], P(('gx', 'gy'))
Inputs may be any that keep to these rules, and one draw needn't show every extreme that they name: `near_ids`: row l names 8 different leaves of a window of 9 consecutive leaves that contains l, centred on l where the ends allow. `leaf_far`: row l names 6 different leaves held by l's device or its two neighbours in leaf order, none within 4 leaves of l; only the first leaf_count[l] entries are used. `leaf_count`: every device holds a leaf with 6. `cluster_far`: row u names 6 different level-two clusters other than u, of u's group or the two groups beside it. `group_far`: row g names 6 different level-one clusters other than g. `geometry`: rows 0 to 2 hold a panel's centre, rows 3 to 5 its unit normal, row 6 its area, from 0.25 to 2.
All inputs are finite; a program needn't handle non-finite values.
Results may differ from a plain program's by a relative error of at most 0.012.
Values may be sent and summed in bfloat16 or wider, within the bound.
A program may use at most 128 MiB of HBM per device.

v0:
```python
import math
import jax
import jax.numpy as jnp
from jax import lax
from jax.sharding import PartitionSpec as P

REACH = 4
BRANCH = 4
four_pi = 4.0 * math.pi
leaf_block = 8


def padded(cells, sides, width):
    for axis, dim in sides:
        count = lax.axis_size(axis)
        ends = count - 1
        head = lax.slice_in_dim(cells, 0, width, axis=dim)
        tail = lax.slice_in_dim(cells, cells.shape[dim] - width, cells.shape[dim], axis=dim)
        cells = jnp.concatenate(
            [
                lax.ppermute(tail, axis, [(i, (i + 1) % count) for i in range(ends)]),
                cells,
                lax.ppermute(head, axis, [((i + 1) % count, i) for i in range(ends)]),
            ],
            axis=dim,
        )
    return cells


def near_kernel(target, source):
    offsets = [
        target[:, coord_id, :, None, None] - source[:, None, :, coord_id, :]
        for coord_id in range(3)
    ]
    distance = offsets[0] * offsets[0] + offsets[1] * offsets[1] + offsets[2] * offsets[2]
    facing = (
        source[:, None, :, 3, :] * offsets[0]
        + source[:, None, :, 4, :] * offsets[1]
        + source[:, None, :, 5, :] * offsets[2]
    )
    panel_area = source[:, None, :, 6, :]
    spread = distance + panel_area
    return panel_area * facing / (four_pi * spread * jnp.sqrt(spread))


def on_device(
    densities,
    geometry,
    near_ids,
    basis_in,
    basis_out,
    leaf_up,
    leaf_down,
    leaf_coupling,
    leaf_far,
    leaf_count,
    cluster_up,
    cluster_down,
    cluster_coupling,
    cluster_far,
    group_up,
    group_down,
    group_coupling,
    group_far,
    root_coupling,
):
    wide = jnp.float32
    narrow = jnp.bfloat16
    leaves = densities.shape[0]
    coeff_order = basis_in.shape[1]
    columns = densities.shape[1]
    flat = coeff_order * columns
    first_leaf = lax.axis_index(("gx", "gy")) * leaves
    gx_index = lax.axis_index("gx")
    group_size = lax.axis_size("gy")
    groups = lax.axis_size("gx")
    leaf_coeffs = jnp.einsum(
        "lkm,lrm->lkr", basis_in, densities, preferred_element_type=wide
    ).astype(narrow)
    mid_coeffs = jnp.einsum(
        "lik,lkr->ir", leaf_up, leaf_coeffs, preferred_element_type=wide
    ).astype(narrow)
    mid_term = jnp.dot(cluster_up[0], mid_coeffs, preferred_element_type=wide).reshape(1, flat)
    mid_flat = mid_coeffs.reshape(1, flat)
    siblings = lax.all_gather(mid_flat, "gy", axis=0, tiled=True)
    group_sum = lax.psum(mid_term, "gy")
    nearby = padded(siblings, (("gx", 0),), group_size)
    mid_picked = jnp.take(nearby, cluster_far[0] - (gx_index - 1) * group_size, axis=0)
    top_coeffs = lax.all_gather(group_sum.astype(narrow), "gx", axis=0, tiled=True)
    top_block = top_coeffs.reshape(groups, coeff_order, columns)
    root_terms = jnp.einsum("gik,gkr->gir", group_up, top_block, preferred_element_type=wide)
    root_coeffs = jnp.sum(
        root_terms.reshape(groups // BRANCH, BRANCH, coeff_order, columns), axis=1
    ).astype(narrow)
    root_row = lax.dynamic_index_in_dim(root_coupling, gx_index // BRANCH, 0, keepdims=False)
    root_field = jnp.einsum(
        "sik,skr->ir", root_row, root_coeffs, preferred_element_type=wide
    ).astype(narrow)
    top_picked = jnp.take(top_block, group_far[0], axis=0)
    top_field = (
        jnp.einsum("fik,fkr->ir", group_coupling[0], top_picked, preferred_element_type=wide)
        + jnp.dot(group_down[0], root_field, preferred_element_type=wide)
    ).astype(narrow)
    mid_block = mid_picked.reshape(-1, coeff_order, columns)
    mid_field = (
        jnp.einsum("fik,fkr->ir", cluster_coupling[0], mid_block, preferred_element_type=wide)
        + jnp.dot(cluster_down[0], top_field, preferred_element_type=wide)
    ).astype(narrow)
    coeff_rim = padded(leaf_coeffs.reshape(leaves, flat), ((("gx", "gy"), 0),), leaves)
    picked = jnp.take(coeff_rim, leaf_far - (first_leaf - leaves), axis=0).reshape(
        leaves, -1, coeff_order, columns
    )
    live_mask = (lax.broadcasted_iota(jnp.int32, leaf_far.shape, 1) < leaf_count[:, None]).astype(
        narrow
    )
    picked = picked * live_mask[:, :, None, None]
    leaf_field = (
        jnp.einsum("lfik,lfkr->lir", leaf_coupling, picked, preferred_element_type=wide)
        + jnp.einsum("lik,kr->lir", leaf_down, mid_field, preferred_element_type=wide)
    ).astype(narrow)
    far_part = jnp.einsum("lkr,lkm->lrm", leaf_field, basis_out, preferred_element_type=wide)
    values_rim = padded(densities, ((("gx", "gy"), 0),), REACH)
    shape_rim = padded(geometry, ((("gx", "gy"), 0),), REACH)
    near_local = near_ids - (first_leaf - REACH)

    def near_block(pieces):
        target, indices = pieces
        source = jnp.take(shape_rim, indices, axis=0)
        values = jnp.take(values_rim, indices, axis=0)
        kernel = near_kernel(target, source).astype(narrow)
        return jnp.einsum("bmnj,bnrj->brm", kernel, values, preferred_element_type=wide)

    near_part = lax.map(
        near_block,
        (
            geometry.reshape(leaves // leaf_block, leaf_block, 7, -1),
            near_local.reshape(leaves // leaf_block, leaf_block, -1),
        ),
    )
    return far_part + near_part.reshape(far_part.shape)


def solution(mesh):
    return jax.shard_map(
        on_device,
        mesh=mesh,
        in_specs=(
            P(("gx", "gy"), None, None),
            P(("gx", "gy"), None, None),
            P(("gx", "gy"), None),
            P(("gx", "gy"), None, None),
            P(("gx", "gy"), None, None),
            P(("gx", "gy"), None, None),
            P(("gx", "gy"), None, None),
            P(("gx", "gy"), None, None, None),
            P(("gx", "gy"), None),
            P(("gx", "gy")),
            P(("gx", "gy"), None, None),
            P(("gx", "gy"), None, None),
            P(("gx", "gy"), None, None, None),
            P(("gx", "gy"), None),
            P(),
            P("gx", None, None),
            P("gx", None, None, None),
            P("gx", None),
            P(),
        ),
        out_specs=P(("gx", "gy"), None, None),
        check_vma=False,
    )
```

profile of v0, /device:TPU:8, one launch (start us, length us, event | category | flops | bytes accessed | tf_op | source)
XLA Modules:
  0.0 328.0 jit_solution(2928487035204301218)
XLA Ops:
  0.0 2.6 convolution_convert_fusion
  2.6 1.3 copy.65
  4.0 1.0 copy.66
  4.9 9.3 %collective-permute-start.1 = (bf16[96,2048]{1,0:T(8,128)(2,1)}, bf16[96,2048]{1,0:T(8,128)(2,1)}, u32[]{:S(2)}, u32[]{:S(2)}) collective-permute-start(bf16[96,2048]{1,0:T(8,128)(2,1)} %copy.66), channel_id=1, source_target_pairs={{1,0},{2,1},{3,2},{4,3},{5,4},{6,5},{7,6},{8,7},{9,8},{10,9},{11,1... | collective-permute-start | bytes 1179656 | tf_op jit(solution)/shard_map/ppermute | solution.py:23
  14.2 1.9 collective-permute-start
  16.2 1.2 copy.80
  17.4 1.9 collective-permute-start.6
  19.3 8.0 %collective-permute-start.7 = (f32[4,7,128]{2,1,0:T(8,128)S(1)}, f32[4,7,128]{2,1,0:T(8,128)S(1)}, u32[]{:S(2)}, u32[]{:S(2)}) collective-permute-start(f32[4,7,128]{2,1,0:T(8,128)S(1)} %get-tuple-element.83), channel_id=1, source_target_pairs={{1,0},{2,1},{3,2},{4,3},{5,4},{6,5},{7,6},{8,7},{9,8},{10,9},{11,1... | collective-permute-start | bytes 43016 | tf_op jit(solution)/shard_map/ppermute | solution.py:23
  27.3 4.0 %copy.72 = bf16[96,64,64]{2,1,0:T(8,128)(2,1)} copy(bf16[96,64,64]{0,2,1:T(8,128)(2,1)} %param.26) | data formatting | bytes 1572864 | tf_op args[5]
  31.4 2.0 fusion.35
  33.5 12.8 %all-gather = bf16[8,1,2048]{2,1,0:T(2,128)(2,1)S(1)} all-gather(bf16[1,1,2048]{2,1,0:T(2,128)(2,1)S(1)} %reshape.240), channel_id=1, replica_groups=mesh['gx'=32,'gy'=8] {'gy'}, dimensions={0}, use_global_device_ids=true | all-gather | bytes 36864 | tf_op jit(solution)/shard_map/all_gather | solution.py:85
  46.3 1.9 collective-permute-start.3
  48.4 0.8 fusion.62
  50.4 24.5 %psum.7 = bf16[1,2048]{1,0:T(2,128)(2,1)S(1)} all-reduce(f32[1,2048]{1,0:T(1,128)S(1)} %reshape.189), channel_id=1, replica_groups=mesh['gx'=32,'gy'=8] {'gy'}, use_global_device_ids=true, to_apply=%region_0.0 | all-reduce | flops 2048 | bytes 12288 | tf_op jit(solution)/shard_map/psum | solution.py:86
  74.9 48.0 %all-gather.1 = bf16[32,1,2048]{2,1,0:T(2,128)(2,1)S(1)} all-gather(bf16[1,1,2048]{2,1,0:T(2,128)(2,1)S(1)} %bitcast.169), channel_id=1, replica_groups=mesh['gx'=32,'gy'=8] {'gx'}, dimensions={0}, use_global_device_ids=true | all-gather | bytes 135168 | tf_op jit(solution)/shard_map/all_gather | solution.py:89
  125.1 1.1 convolution_bitcast_fusion.1
  126.2 1.8 fusion.33
  129.4 4.0 %copy.78 = bf16[96,64,64]{2,1,0:T(8,128)(2,1)} copy(bf16[96,64,64]{0,2,1:T(8,128)(2,1)} %param.27) | data formatting | bytes 1572864 | tf_op args[6]
  133.4 16.1 %copy.71 = bf16[96,6,64,64]{3,2,1,0:T(8,128)(2,1)} copy(bf16[96,6,64,64]{0,3,2,1:T(8,128)(2,1)} %param.28) | data formatting | bytes 9437184 | tf_op args[7]
  149.5 2.4 collective-permute-start.2
  152.0 1.9 collective-permute-start.4
  154.0 8.0 %collective-permute-start.5 = (bf16[4,32,128]{2,1,0:T(8,128)(2,1)S(1)}, bf16[4,32,128]{2,1,0:T(8,128)(2,1)S(1)}, u32[]{:S(2)}, u32[]{:S(2)}) collective-permute-start(bf16[4,32,128]{2,1,0:T(8,128)(2,1)S(1)} %get-tuple-element.81), channel_id=1, source_target_pairs={{1,0},{2,1},{3,2},{4,3},{5,4},{6,5},{7,6},{8,7},{9,8},{10,9},{11,1... | collective-permute-start | bytes 98312 | tf_op jit(solution)/shard_map/ppermute | solution.py:23
  163.5 1.2 pad_maximum_fusion.1
  164.7 130.7 %while.10 = (s32[]{:T(128)}, f32[12,8,32,128]{3,2,1,0:T(8,128)}, s32[12,8,8]{2,1,0:T(8,128)}, bf16[104,32,128]{2,1,0:T(8,128)(2,1)S(1)}, f32[104,7,128]{2,1,0:T(...) while((s32[]{:T(128)}, f32[12,8,32,128]{3,2,1,0:T(8,128)}, s32[12,8,8]{2,1,0:T(8,128)}, ...), condition=%wide.region_3.4_spmd, body=%wide.region_2.3_spmd.sunk | while | flops 87352896 | bytes 3410213 | solution.py:133
  168.3 0.8 fusion.83
  169.7 5.9 %fusion.84 = f32[12,8,32,128]{3,2,1,0:T(8,128)} fusion(f32[12,8,32,128]{3,2,1,0:T(8,128)} %get-tuple-element.149, s32[]{:T(128)S(6)} %copy.97, f32[8,8,128]{2,1,0:T(8,128)S(1)} %bitcast.159, f32[8,128]{1,0:T(8,128)} %get-tuple-element.132, f32[8,8,128]{2,1,0:T(8,128)S(1)} %bitcast.160, f32[8,8,128]{2,1,0:T(8,128)S(1)} %bitcast.161, ...), kind=kOutput, calls=%fused_computation.21.clone.1 | convolution fusion | flops 87293952 | bytes 897092 | tf_op jit(solution)/shard_map/while/body/eval_jaxpr/bmnj,bnrj->brm/dot_general | solution.py:131
  179.2 0.8 fusion.83
  180.6 5.9 %fusion.84 = f32[12,8,32,128]{3,2,1,0:T(8,128)} fusion(f32[12,8,32,128]{3,2,1,0:T(8,128)} %get-tuple-element.149, s32[]{:T(128)S(6)} %copy.97, f32[8,8,128]{2,1,0:T(8,128)S(1)} %bitcast.159, f32[8,128]{1,0:T(8,128)} %get-tuple-element.132, f32[8,8,128]{2,1,0:T(8,128)S(1)} %bitcast.160, f32[8,8,128]{2,1,0:T(8,128)S(1)} %bitcast.161, ...), kind=kOutput, calls=%fused_computation.21.clone.1 | convolution fusion | flops 87293952 | bytes 897092 | tf_op jit(solution)/shard_map/while/body/eval_jaxpr/bmnj,bnrj->brm/dot_general | solution.py:131
  190.1 0.8 fusion.83
  191.5 5.9 %fusion.84 = f32[12,8,32,128]{3,2,1,0:T(8,128)} fusion(f32[12,8,32,128]{3,2,1,0:T(8,128)} %get-tuple-element.149, s32[]{:T(128)S(6)} %copy.97, f32[8,8,128]{2,1,0:T(8,128)S(1)} %bitcast.159, f32[8,128]{1,0:T(8,128)} %get-tuple-element.132, f32[8,8,128]{2,1,0:T(8,128)S(1)} %bitcast.160, f32[8,8,128]{2,1,0:T(8,128)S(1)} %bitcast.161, ...), kind=kOutput, calls=%fused_computation.21.clone.1 | convolution fusion | flops 87293952 | bytes 897092 | tf_op jit(solution)/shard_map/while/body/eval_jaxpr/bmnj,bnrj->brm/dot_general | solution.py:131
  201.0 0.8 fusion.83
  202.4 5.9 %fusion.84 = f32[12,8,32,128]{3,2,1,0:T(8,128)} fusion(f32[12,8,32,128]{3,2,1,0:T(8,128)} %get-tuple-element.149, s32[]{:T(128)S(6)} %copy.97, f32[8,8,128]{2,1,0:T(8,128)S(1)} %bitcast.159, f32[8,128]{1,0:T(8,128)} %get-tuple-element.132, f32[8,8,128]{2,1,0:T(8,128)S(1)} %bitcast.160, f32[8,8,128]{2,1,0:T(8,128)S(1)} %bitcast.161, ...), kind=kOutput, calls=%fused_computation.21.clone.1 | convolution fusion | flops 87293952 | bytes 897092 | tf_op jit(solution)/shard_map/while/body/eval_jaxpr/bmnj,bnrj->brm/dot_general | solution.py:131
  211.9 0.8 fusion.83
  213.3 5.9 %fusion.84 = f32[12,8,32,128]{3,2,1,0:T(8,128)} fusion(f32[12,8,32,128]{3,2,1,0:T(8,128)} %get-tuple-element.149, s32[]{:T(128)S(6)} %copy.97, f32[8,8,128]{2,1,0:T(8,128)S(1)} %bitcast.159, f32[8,128]{1,0:T(8,128)} %get-tuple-element.132, f32[8,8,128]{2,1,0:T(8,128)S(1)} %bitcast.160, f32[8,8,128]{2,1,0:T(8,128)S(1)} %bitcast.161, ...), kind=kOutput, calls=%fused_computation.21.clone.1 | convolution fusion | flops 87293952 | bytes 897092 | tf_op jit(solution)/shard_map/while/body/eval_jaxpr/bmnj,bnrj->brm/dot_general | solution.py:131
  224.2 5.9 %fusion.84 = f32[12,8,32,128]{3,2,1,0:T(8,128)} fusion(f32[12,8,32,128]{3,2,1,0:T(8,128)} %get-tuple-element.149, s32[]{:T(128)S(6)} %copy.97, f32[8,8,128]{2,1,0:T(8,128)S(1)} %bitcast.159, f32[8,128]{1,0:T(8,128)} %get-tuple-element.132, f32[8,8,128]{2,1,0:T(8,128)S(1)} %bitcast.160, f32[8,8,128]{2,1,0:T(8,128)S(1)} %bitcast.161, ...), kind=kOutput, calls=%fused_computation.21.clone.1 | convolution fusion | flops 87293952 | bytes 897092 | tf_op jit(solution)/shard_map/while/body/eval_jaxpr/bmnj,bnrj->brm/dot_general | solution.py:131
  235.1 5.9 %fusion.84 = f32[12,8,32,128]{3,2,1,0:T(8,128)} fusion(f32[12,8,32,128]{3,2,1,0:T(8,128)} %get-tuple-element.149, s32[]{:T(128)S(6)} %copy.97, f32[8,8,128]{2,1,0:T(8,128)S(1)} %bitcast.159, f32[8,128]{1,0:T(8,128)} %get-tuple-element.132, f32[8,8,128]{2,1,0:T(8,128)S(1)} %bitcast.160, f32[8,8,128]{2,1,0:T(8,128)S(1)} %bitcast.161, ...), kind=kOutput, calls=%fused_computation.21.clone.1 | convolution fusion | flops 87293952 | bytes 897092 | tf_op jit(solution)/shard_map/while/body/eval_jaxpr/bmnj,bnrj->brm/dot_general | solution.py:131
  246.0 5.9 %fusion.84 = f32[12,8,32,128]{3,2,1,0:T(8,128)} fusion(f32[12,8,32,128]{3,2,1,0:T(8,128)} %get-tuple-element.149, s32[]{:T(128)S(6)} %copy.97, f32[8,8,128]{2,1,0:T(8,128)S(1)} %bitcast.159, f32[8,128]{1,0:T(8,128)} %get-tuple-element.132, f32[8,8,128]{2,1,0:T(8,128)S(1)} %bitcast.160, f32[8,8,128]{2,1,0:T(8,128)S(1)} %bitcast.161, ...), kind=kOutput, calls=%fused_computation.21.clone.1 | convolution fusion | flops 87293952 | bytes 897092 | tf_op jit(solution)/shard_map/while/body/eval_jaxpr/bmnj,bnrj->brm/dot_general | solution.py:131
  255.4 0.8 fusion.83
  256.9 5.9 %fusion.84 = f32[12,8,32,128]{3,2,1,0:T(8,128)} fusion(f32[12,8,32,128]{3,2,1,0:T(8,128)} %get-tuple-element.149, s32[]{:T(128)S(6)} %copy.97, f32[8,8,128]{2,1,0:T(8,128)S(1)} %bitcast.159, f32[8,128]{1,0:T(8,128)} %get-tuple-element.132, f32[8,8,128]{2,1,0:T(8,128)S(1)} %bitcast.160, f32[8,8,128]{2,1,0:T(8,128)S(1)} %bitcast.161, ...), kind=kOutput, calls=%fused_computation.21.clone.1 | convolution fusion | flops 87293952 | bytes 897092 | tf_op jit(solution)/shard_map/while/body/eval_jaxpr/bmnj,bnrj->brm/dot_general | solution.py:131
  267.8 5.9 %fusion.84 = f32[12,8,32,128]{3,2,1,0:T(8,128)} fusion(f32[12,8,32,128]{3,2,1,0:T(8,128)} %get-tuple-element.149, s32[]{:T(128)S(6)} %copy.97, f32[8,8,128]{2,1,0:T(8,128)S(1)} %bitcast.159, f32[8,128]{1,0:T(8,128)} %get-tuple-element.132, f32[8,8,128]{2,1,0:T(8,128)S(1)} %bitcast.160, f32[8,8,128]{2,1,0:T(8,128)S(1)} %bitcast.161, ...), kind=kOutput, calls=%fused_computation.21.clone.1 | convolution fusion | flops 87293952 | bytes 897092 | tf_op jit(solution)/shard_map/while/body/eval_jaxpr/bmnj,bnrj->brm/dot_general | solution.py:131
  278.7 5.9 %fusion.84 = f32[12,8,32,128]{3,2,1,0:T(8,128)} fusion(f32[12,8,32,128]{3,2,1,0:T(8,128)} %get-tuple-element.149, s32[]{:T(128)S(6)} %copy.97, f32[8,8,128]{2,1,0:T(8,128)S(1)} %bitcast.159, f32[8,128]{1,0:T(8,128)} %get-tuple-element.132, f32[8,8,128]{2,1,0:T(8,128)S(1)} %bitcast.160, f32[8,8,128]{2,1,0:T(8,128)S(1)} %bitcast.161, ...), kind=kOutput, calls=%fused_computation.21.clone.1 | convolution fusion | flops 87293952 | bytes 897092 | tf_op jit(solution)/shard_map/while/body/eval_jaxpr/bmnj,bnrj->brm/dot_general | solution.py:131
  289.6 5.9 %fusion.84 = f32[12,8,32,128]{3,2,1,0:T(8,128)} fusion(f32[12,8,32,128]{3,2,1,0:T(8,128)} %get-tuple-element.149, s32[]{:T(128)S(6)} %copy.97, f32[8,8,128]{2,1,0:T(8,128)S(1)} %bitcast.159, f32[8,128]{1,0:T(8,128)} %get-tuple-element.132, f32[8,8,128]{2,1,0:T(8,128)S(1)} %bitcast.160, f32[8,8,128]{2,1,0:T(8,128)S(1)} %bitcast.161, ...), kind=kOutput, calls=%fused_computation.21.clone.1 | convolution fusion | flops 87293952 | bytes 897092 | tf_op jit(solution)/shard_map/while/body/eval_jaxpr/bmnj,bnrj->brm/dot_general | solution.py:131
  295.4 1.1 convolution_bitcast_fusion.3
  296.5 4.3 %fusion.37 = f32[32,96,64]{2,0,1:T(8,128)} fusion(bf16[96,64,64]{2,1,0:T(8,128)(2,1)} %copy.78, f32[32,64]{1,0:T(8,128)S(1)} %convolution_bitcast_fusion.3, bf16[32,64]{1,0:T(8,128)(2,1)} %fusion.33, bf16[1,64,64]{2,1,0:T(8,128)(2,1)} %param.32), kind=kOutput, calls=%fused_computation.60 | convolution fusion | flops 25432064 | bytes 1593344 | tf_op jit(solution)/shard_map/lik,kr->lir/dot_general | solution.py:119
  300.8 1.3 pad_maximum_fusion
  302.1 4.0 %gather_fusion.2 = bf16[576,2048]{1,0:T(8,128)(2,1)} fusion(bf16[288,2048]{1,0:T(8,128)(2,1)S(1)} %pad_maximum_fusion, s32[1024]{0:T(1024)S(1)} %pad_clamp_fusion.3), kind=kCustom, calls=%fused_computation.2 | custom fusion | bytes 4720896 | tf_op jit(solution)/shard_map/jit(_take)/gather | solution.py:110
  306.1 11.7 %gather.23 = bf16[96,6,64,32]{3,2,1,0:T(8,128)(2,1)} reshape(bf16[576,2048]{1,0:T(8,128)(2,1)} %gather_fusion.2) | data formatting | bytes 4718592 | tf_op jit(solution)/shard_map/jit(_take)/gather | solution.py:110
  317.8 10.3 %bitcast_add_fusion.1 = f32[96,32,128]{2,1,0:T(8,128)} fusion(f32[12,8,32,128]{3,2,1,0:T(8,128)} %get-tuple-element.37, bf16[96,64,128]{2,1,0:T(8,128)(2,1)S(1)} %copy-done, f32[32,96,64]{2,0,1:T(8,128)S(1)} %copy-done.1, bf16[96,6,64,64]{3,2,1,0:T(8,128)(2,1)} %copy.71, bf16[96,6,64,32]{3,2,1,0:T(8,128)(2,1)} %gather.23, pred[96,6]{1,0:T(8,128)(4,1)S(1)} %copy-done.6, ...), kind=kOutput, calls=%fused_computation.44 | convolution fusion | flops 204472320 | bytes 12584640 | tf_op jit(solution)/shard_map/lkr,lkm->lrm/dot_general | solution.py:121
  (177 shorter events, 61.8 us)
Async XLA Ops:
  0.0 317.8 %copy-start = (bf16[96,64,128]{2,1,0:T(8,128)(2,1)S(1)}, bf16[96,64,128]{2,1,0:T(8,128)(2,1)}, u32[]{:S(2)}) copy-start(bf16[96,64,128]{2,1,0:T(8,128)(2,1)} %param.25) | copy-start | bytes 4718596
  4.9 295.9 %collective-permute-start.1 = (bf16[96,2048]{1,0:T(8,128)(2,1)}, bf16[96,2048]{1,0:T(8,128)(2,1)}, u32[]{:S(2)}, u32[]{:S(2)}) collective-permute-start(bf16[96,2048]{1,0:T(8,128)(2,1)} %copy.66), channel_id=1, source_target_pairs={{1,0},{2,1},{3,2},{4,3},{5,4},{6,5},{7,6},{8,7},{9,8},{10,9},{11,1... | collective-permute-start | bytes 1179656 | tf_op jit(solution)/shard_map/ppermute | solution.py:23
  14.2 286.6 %collective-permute-start = (bf16[96,2048]{1,0:T(8,128)(2,1)}, bf16[96,2048]{1,0:T(8,128)(2,1)}, u32[]{:S(2)}, u32[]{:S(2)}) collective-permute-start(bf16[96,2048]{1,0:T(8,128)(2,1)} %copy.66), channel_id=1, source_target_pairs={{0,1},{1,2},{2,3},{3,4},{4,5},{5,6},{6,7},{7,8},{8,9},{9,10},{10,1... | collective-permute-start | bytes 1179656 | tf_op jit(solution)/shard_map/ppermute | solution.py:21
  17.4 132.2 %collective-permute-start.6 = (f32[4,7,128]{2,1,0:T(8,128)S(1)}, f32[4,7,128]{2,1,0:T(8,128)S(1)}, u32[]{:S(2)}, u32[]{:S(2)}) collective-permute-start(f32[4,7,128]{2,1,0:T(8,128)S(1)} %get-tuple-element.82), channel_id=1, source_target_pairs={{0,1},{1,2},{2,3},{3,4},{4,5},{5,6},{6,7},{7,8},{8,9},{9,10},{10,1... | collective-permute-start | bytes 43016 | tf_op jit(solution)/shard_map/ppermute | solution.py:21
  19.3 29.0 %copy-start.10 = (s32[1,6]{1,0:T(1,128)S(1)}, s32[1,6]{1,0:T(1,128)}, u32[]{:S(2)}) copy-start(s32[1,6]{1,0:T(1,128)} %param.34) | copy-start | bytes 76
  19.3 29.0 %copy-start.11 = (s32[1,6]{1,0:T(1,128)S(1)}, s32[1,6]{1,0:T(1,128)}, u32[]{:S(2)}) copy-start(s32[1,6]{1,0:T(1,128)} %param.38) | copy-start | bytes 76
  19.3 29.8 %copy-start.9 = (s32[96]{0:T(128)S(1)}, s32[96]{0:T(128)}, u32[]{:S(2)}) copy-start(s32[96]{0:T(128)} %param.30) | copy-start | bytes 1156
  19.3 30.5 %copy-start.7 = (s32[96,6]{0,1:T(8,128)S(1)}, s32[96,6]{0,1:T(8,128)}, u32[]{:S(2)}) copy-start(s32[96,6]{0,1:T(8,128)} %param.29) | copy-start | bytes 6916
  19.3 30.8 %copy-start.4 = (bf16[1,64,64]{2,1,0:T(8,128)(2,1)S(1)}, bf16[1,64,64]{2,1,0:T(8,128)(2,1)}, u32[]{:S(2)}) copy-start(bf16[1,64,64]{2,1,0:T(8,128)(2,1)} %param.31) | copy-start | bytes 24580
  19.3 132.6 %collective-permute-start.7 = (f32[4,7,128]{2,1,0:T(8,128)S(1)}, f32[4,7,128]{2,1,0:T(8,128)S(1)}, u32[]{:S(2)}, u32[]{:S(2)}) collective-permute-start(f32[4,7,128]{2,1,0:T(8,128)S(1)} %get-tuple-element.83), channel_id=1, source_target_pairs={{1,0},{2,1},{3,2},{4,3},{5,4},{6,5},{7,6},{8,7},{9,8},{10,9},{11,1... | collective-permute-start | bytes 43016 | tf_op jit(solution)/shard_map/ppermute | solution.py:23
  31.4 92.7 %copy-start.2 = (bf16[32,64,64]{2,1,0:T(8,128)(2,1)S(1)}, bf16[32,64,64]{2,1,0:T(8,128)(2,1)}, u32[]{:S(2)}) copy-start(bf16[32,64,64]{2,1,0:T(8,128)(2,1)} %param.35) | copy-start | bytes 786436
  31.4 93.7 %copy-start.8 = (s32[96,8]{0,1:T(8,128)S(1)}, s32[96,8]{0,1:T(8,128)}, u32[]{:S(2)}) copy-start(s32[96,8]{0,1:T(8,128)} %param.23) | copy-start | bytes 9220
  33.3 92.9 %copy-start.5 = (bf16[1,64,64]{2,1,0:T(8,128)(2,1)S(1)}, bf16[1,64,64]{2,1,0:T(8,128)(2,1)}, u32[]{:S(2)}) copy-start(bf16[1,64,64]{2,1,0:T(8,128)(2,1)} %param.36) | copy-start | bytes 24580
  46.3 107.6 %collective-permute-start.3 = (bf16[8,2048]{1,0:T(8,128)(2,1)S(1)}, bf16[8,2048]{1,0:T(8,128)(2,1)S(1)}, u32[]{:S(2)}, u32[]{:S(2)}) collective-permute-start(bf16[8,2048]{1,0:T(8,128)(2,1)S(1)} %bitcast.165), channel_id=1, source_target_pairs={{8,0},{16,8},{24,16},{32,24},{40,32},{48,40},{56,48},{64,56},{72,6... | collective-permute-start | bytes 98312 | tf_op jit(solution)/shard_map/ppermute | solution.py:23
  149.5 12.5 %collective-permute-start.2 = (bf16[8,2048]{1,0:T(8,128)(2,1)S(1)}, bf16[8,2048]{1,0:T(8,128)(2,1)S(1)}, u32[]{:S(2)}, u32[]{:S(2)}) collective-permute-start(bf16[8,2048]{1,0:T(8,128)(2,1)S(1)} %bitcast.166), channel_id=1, source_target_pairs={{0,8},{8,16},{16,24},{24,32},{32,40},{40,48},{48,56},{56,64},{64,7... | collective-permute-start | bytes 98312 | tf_op jit(solution)/shard_map/ppermute | solution.py:21
  152.0 11.5 %collective-permute-start.4 = (bf16[4,32,128]{2,1,0:T(8,128)(2,1)S(1)}, bf16[4,32,128]{2,1,0:T(8,128)(2,1)S(1)}, u32[]{:S(2)}, u32[]{:S(2)}) collective-permute-start(bf16[4,32,128]{2,1,0:T(8,128)(2,1)S(1)} %get-tuple-element.80), channel_id=1, source_target_pairs={{0,1},{1,2},{2,3},{3,4},{4,5},{5,6},{6,7},{7,8},{8,9},{9,10},{10,1... | collective-permute-start | bytes 98312 | tf_op jit(solution)/shard_map/ppermute | solution.py:21
  154.0 9.5 %collective-permute-start.5 = (bf16[4,32,128]{2,1,0:T(8,128)(2,1)S(1)}, bf16[4,32,128]{2,1,0:T(8,128)(2,1)S(1)}, u32[]{:S(2)}, u32[]{:S(2)}) collective-permute-start(bf16[4,32,128]{2,1,0:T(8,128)(2,1)S(1)} %get-tuple-element.81), channel_id=1, source_target_pairs={{1,0},{2,1},{3,2},{4,3},{5,4},{6,5},{7,6},{8,7},{9,8},{10,9},{11,1... | collective-permute-start | bytes 98312 | tf_op jit(solution)/shard_map/ppermute | solution.py:23
  306.1 11.7 %copy-start.1 = (f32[32,96,64]{2,0,1:T(8,128)S(1)}, f32[32,96,64]{2,0,1:T(8,128)}, u32[]{:S(2)}) copy-start(f32[32,96,64]{2,0,1:T(8,128)} %fusion.37) | copy-start | bytes 2359300
  306.1 11.7 %copy-start.3 = (bf16[96,6]{1,0:T(8,128)(2,1)S(1)}, bf16[96,6]{1,0:T(8,128)(2,1)}, u32[]{:S(2)}) copy-start(bf16[96,6]{1,0:T(8,128)(2,1)} %fusion.49) | copy-start | bytes 3460
  306.1 11.7 %copy-start.6 = (pred[96,6]{1,0:T(8,128)(4,1)S(1)}, pred[96,6]{1,0:T(8,128)(4,1)}, u32[]{:S(2)}) copy-start(pred[96,6]{1,0:T(8,128)(4,1)} %copy.64) | copy-start | bytes 1732
where the time goes:
time: 331 us; the launch traced here: 328 us
  matrix products  94.2 us (28%)
  local copies, waits for them, and re-layouts  90.2 us (27%)
  blocking collectives  85.2 us (26%)
  starting transfers between devices  35.4 us (11%)
  other arithmetic  22.2 us (7%)
    dot_general x12, matrix products, near_block(): jnp.einsum('bmnj,bnrj->brm', kernel, values, preferred_element_type=wide)  70.5 us
    all_gather x1, blocking collectives, on_device(): lax.all_gather(group_sum.astype(narrow), 'gx', axis=0, tiled=True)  48 us
    ppermute x4, starting transfers between devices, padded(): lax.ppermute(head, axis, [((i + 1) % count, i) for i in range(ends)])  27.2 us
    unnamed x30, local copies, waits for them, and re-layouts  25.5 us
    psum x1, blocking collectives, on_device(): group_sum = lax.psum(mid_term, 'gy')  24.5 us
    gather x2, local copies, waits for them, and re-layouts, on_device(): jnp.take(coeff_rim, leaf_far - (first_leaf - leaves), axis=0)  15.6 us
    all_gather x1, blocking collectives, on_device(): siblings = lax.all_gather(mid_flat, 'gy', axis=0, tiled=True)  12.8 us
    dot_general x1, matrix products, on_device(): jnp.einsum('lkr,lkm->lrm', leaf_field, basis_out, preferred_element_type=...  10.3 us
  transfers between devices with their start and end apart: 8, of which 0 were waited for; matrix products, arithmetic and copies ran while one was open for 53% of the time, Pallas kernels for 0%

commit v1 on v0

--- a/solution.py
+++ b/solution.py
@@ -8,6 +8,19 @@
 BRANCH = 4
 four_pi = 4.0 * math.pi
 leaf_block = 8
+
+
+def _supply_set(here_x, named_axis):
+    piece_out = jnp.concatenate(
+        lax.all_to_all(
+            jnp.stack(tuple((here_x for _ in range(lax.axis_size(named_axis))))),
+            axis_name=named_axis,
+            split_axis=0,
+            concat_axis=0,
+        ),
+        axis=0,
+    )
+    return piece_out
 
 
 def padded(cells, sides, width):
@@ -86,7 +99,7 @@
     group_sum = lax.psum(mid_term, "gy")
     nearby = padded(siblings, (("gx", 0),), group_size)
     mid_picked = jnp.take(nearby, cluster_far[0] - (gx_index - 1) * group_size, axis=0)
-    top_coeffs = lax.all_gather(group_sum.astype(narrow), "gx", axis=0, tiled=True)
+    top_coeffs = _supply_set(group_sum.astype(narrow), "gx")
     top_block = top_coeffs.reshape(groups, coeff_order, columns)
     root_terms = jnp.einsum("gik,gkr->gir", group_up, top_block, preferred_element_type=wide)
     root_coeffs = jnp.sum(

time: 331 us -> 296 us (0.89)
  blocking collectives: 85.2 us -> 36.7 us
  other arithmetic: 22.2 us -> 27.5 us
  local copies, waits for them, and re-layouts: 90.2 us -> 95 us
    all_gather x1 -> x0, blocking collectives: 48 us -> none  [on_device(): lax.all_gather(group_sum.astype(narrow), 'gx', axis=0, tiled=True)]
    all_to_all x0 -> x1, starting transfers between devices: none -> 5.65 us  [_supply_set(): lax.all_to_all(jnp.stack(tuple((here_x for _ in range(lax.axis_size(named...]
    unnamed x30 -> x36, local copies, waits for them, and re-layouts: 25.5 us -> 28.2 us
  transfers between devices with their start and end apart: 8 -> 9, of which waited for: 0 -> 0; matrix products, arithmetic and copies ran while one was open for 53% -> 63% of each run, Pallas kernels for 0% -> 0%
where the time goes in v1:
time: 296 us; the launch traced here: 292 us
  local copies, waits for them, and re-layouts  95 us (32%)
  matrix products  94 us (32%)
  starting transfers between devices  38.5 us (13%)
  blocking collectives  36.7 us (12%)
  other arithmetic  27.5 us (9%)
    dot_general x12, matrix products, near_block(): jnp.einsum('bmnj,bnrj->brm', kernel, values, preferred_element_type=wide)  70.5 us
    unnamed x36, local copies, waits for them, and re-layouts  28.2 us
    ppermute x4, starting transfers between devices, padded(): lax.ppermute(head, axis, [((i + 1) % count, i) for i in range(ends)])  24.5 us
    psum x1, blocking collectives, on_device(): group_sum = lax.psum(mid_term, 'gy')  23.9 us
    gather x2, local copies, waits for them, and re-layouts, on_device(): jnp.take(coeff_rim, leaf_far - (first_leaf - leaves), axis=0)  15.6 us
    all_gather x1, blocking collectives, on_device(): siblings = lax.all_gather(mid_flat, 'gy', axis=0, tiled=True)  12.8 us
    dot_general x1, matrix products, on_device(): jnp.einsum('lkr,lkm->lrm', leaf_field, basis_out, preferred_element_type=...  10.3 us
    slice x12, local copies, waits for them, and re-layouts, near_kernel(): panel_area = source[:, None, :, 6, :]  9.31 us
  transfers between devices with their start and end apart: 9, of which 0 were waited for; matrix products, arithmetic and copies ran while one was open for 63% of the time, Pallas kernels for 0%

profile of v1, /device:TPU:8, one launch (start us, length us, event | category | flops | bytes accessed | tf_op | source)
XLA Modules:
  0.0 292.4 jit_solution(941053071900236881)
XLA Ops:
  0.0 2.6 convolution_convert_fusion
  2.6 1.3 copy.65
  4.0 0.9 copy.66
  4.9 9.3 %collective-permute-start.1 = (bf16[96,2048]{1,0:T(8,128)(2,1)}, bf16[96,2048]{1,0:T(8,128)(2,1)}, u32[]{:S(2)}, u32[]{:S(2)}) collective-permute-start(bf16[96,2048]{1,0:T(8,128)(2,1)} %copy.66), channel_id=1, source_target_pairs={{1,0},{2,1},{3,2},{4,3},{5,4},{6,5},{7,6},{8,7},{9,8},{10,9},{11,1... | collective-permute-start | bytes 1179656 | tf_op jit(solution)/shard_map/ppermute | solution.py:36
  14.2 1.9 collective-permute-start
  16.1 0.8 fusion.62
  16.9 1.9 collective-permute-start.4
  18.8 1.2 copy.80
  20.0 1.9 collective-permute-start.6
  22.0 7.9 %collective-permute-start.7 = (f32[4,7,128]{2,1,0:T(8,128)S(1)}, f32[4,7,128]{2,1,0:T(8,128)S(1)}, u32[]{:S(2)}, u32[]{:S(2)}) collective-permute-start(f32[4,7,128]{2,1,0:T(8,128)S(1)} %get-tuple-element.83), channel_id=1, source_target_pairs={{1,0},{2,1},{3,2},{4,3},{5,4},{6,5},{7,6},{8,7},{9,8},{10,9},{11,1... | collective-permute-start | bytes 43016 | tf_op jit(solution)/shard_map/ppermute | solution.py:36
  29.8 4.0 %copy.72 = bf16[96,64,64]{2,1,0:T(8,128)(2,1)} copy(bf16[96,64,64]{0,2,1:T(8,128)(2,1)} %param.26) | data formatting | bytes 1572864 | tf_op args[5]
  33.9 2.0 fusion.35
  36.2 23.9 %psum.7 = bf16[1,2048]{1,0:T(2,128)(2,1)S(1)} all-reduce(f32[1,2048]{1,0:T(1,128)S(1)} %reshape.189), channel_id=1, replica_groups=mesh['gx'=32,'gy'=8] {'gy'}, use_global_device_ids=true, to_apply=%region_0.0 | all-reduce | flops 2048 | bytes 12288 | tf_op jit(solution)/shard_map/psum | solution.py:99
  60.8 1.4 reduce.3
  62.9 5.6 %all-to-all-start = ((bf16[32,2,1024]{2,1,0:T(2,128)(2,1)}), bf16[32,2,1024]{2,1,0:T(2,128)(2,1)}, u32[]{:S(2)}, u32[]{:S(2)}) async-start(bf16[32,2,1024]{2,1,0:T(2,128)(2,1)} %reshape.251), calls=%async_computation | async-start | bytes 262144 | tf_op jit(solution)/shard_map/all_to_all | solution.py:15
  73.6 12.8 %all-gather = bf16[8,1,2048]{2,1,0:T(2,128)(2,1)S(1)} all-gather(bf16[1,1,2048]{2,1,0:T(2,128)(2,1)S(1)} %reshape.239), channel_id=1, replica_groups=mesh['gx'=32,'gy'=8] {'gy'}, dimensions={0}, use_global_device_ids=true | all-gather | bytes 36864 | tf_op jit(solution)/shard_map/all_gather | solution.py:98
  86.9 4.0 %copy.78 = bf16[96,64,64]{2,1,0:T(8,128)(2,1)} copy(bf16[96,64,64]{0,2,1:T(8,128)(2,1)} %param.27) | data formatting | bytes 1572864 | tf_op args[6]
  90.9 16.1 %copy.71 = bf16[96,6,64,64]{3,2,1,0:T(8,128)(2,1)} copy(bf16[96,6,64,64]{0,3,2,1:T(8,128)(2,1)} %param.28) | data formatting | bytes 9437184 | tf_op args[7]
  107.0 4.0 %collective-permute-start.5 = (bf16[4,32,128]{2,1,0:T(8,128)(2,1)S(1)}, bf16[4,32,128]{2,1,0:T(8,128)(2,1)S(1)}, u32[]{:S(2)}, u32[]{:S(2)}) collective-permute-start(bf16[4,32,128]{2,1,0:T(8,128)(2,1)S(1)} %get-tuple-element.81), channel_id=1, source_target_pairs={{1,0},{2,1},{3,2},{4,3},{5,4},{6,5},{7,6},{8,7},{9,8},{10,9},{11,1... | collective-permute-start | bytes 98312 | tf_op jit(solution)/shard_map/ppermute | solution.py:36
  111.0 3.4 %collective-permute-start.3 = (bf16[8,2048]{1,0:T(8,128)(2,1)}, bf16[8,2048]{1,0:T(8,128)(2,1)}, u32[]{:S(2)}, u32[]{:S(2)}) collective-permute-start(bf16[8,2048]{1,0:T(8,128)(2,1)} %bitcast.123), channel_id=1, source_target_pairs={{8,0},{16,8},{24,16},{32,24},{40,32},{48,40},{56,48},{64,56},{72,6... | collective-permute-start | bytes 98312 | tf_op jit(solution)/shard_map/ppermute | solution.py:36
  114.4 2.7 collective-permute-start.2
  117.1 1.2 pad_maximum_fusion.1
  118.4 130.7 %while.10 = (s32[]{:T(128)}, f32[12,8,32,128]{3,2,1,0:T(8,128)}, s32[12,8,8]{2,1,0:T(8,128)}, bf16[104,32,128]{2,1,0:T(8,128)(2,1)S(1)}, f32[104,7,128]{2,1,0:T(...) while((s32[]{:T(128)}, f32[12,8,32,128]{3,2,1,0:T(8,128)}, s32[12,8,8]{2,1,0:T(8,128)}, ...), condition=%wide.region_3.4_spmd, body=%wide.region_2.3_spmd.sunk | while | flops 87352896 | bytes 3410213 | solution.py:146
  123.4 5.9 %fusion.84 = f32[12,8,32,128]{3,2,1,0:T(8,128)} fusion(f32[12,8,32,128]{3,2,1,0:T(8,128)} %get-tuple-element.149, s32[]{:T(128)S(6)} %copy.97, f32[8,8,128]{2,1,0:T(8,128)S(1)} %bitcast.156, f32[8,128]{1,0:T(8,128)} %get-tuple-element.132, f32[8,8,128]{2,1,0:T(8,128)S(1)} %bitcast.157, f32[8,8,128]{2,1,0:T(8,128)S(1)} %bitcast.158, ...), kind=kOutput, calls=%fused_computation.21.clone.1 | convolution fusion | flops 87293952 | bytes 897092 | tf_op jit(solution)/shard_map/while/body/eval_jaxpr/bmnj,bnrj->brm/dot_general | solution.py:144
  134.3 5.9 %fusion.84 = f32[12,8,32,128]{3,2,1,0:T(8,128)} fusion(f32[12,8,32,128]{3,2,1,0:T(8,128)} %get-tuple-element.149, s32[]{:T(128)S(6)} %copy.97, f32[8,8,128]{2,1,0:T(8,128)S(1)} %bitcast.156, f32[8,128]{1,0:T(8,128)} %get-tuple-element.132, f32[8,8,128]{2,1,0:T(8,128)S(1)} %bitcast.157, f32[8,8,128]{2,1,0:T(8,128)S(1)} %bitcast.158, ...), kind=kOutput, calls=%fused_computation.21.clone.1 | convolution fusion | flops 87293952 | bytes 897092 | tf_op jit(solution)/shard_map/while/body/eval_jaxpr/bmnj,bnrj->brm/dot_general | solution.py:144
  145.2 5.9 %fusion.84 = f32[12,8,32,128]{3,2,1,0:T(8,128)} fusion(f32[12,8,32,128]{3,2,1,0:T(8,128)} %get-tuple-element.149, s32[]{:T(128)S(6)} %copy.97, f32[8,8,128]{2,1,0:T(8,128)S(1)} %bitcast.156, f32[8,128]{1,0:T(8,128)} %get-tuple-element.132, f32[8,8,128]{2,1,0:T(8,128)S(1)} %bitcast.157, f32[8,8,128]{2,1,0:T(8,128)S(1)} %bitcast.158, ...), kind=kOutput, calls=%fused_computation.21.clone.1 | convolution fusion | flops 87293952 | bytes 897092 | tf_op jit(solution)/shard_map/while/body/eval_jaxpr/bmnj,bnrj->brm/dot_general | solution.py:144
  156.1 5.9 %fusion.84 = f32[12,8,32,128]{3,2,1,0:T(8,128)} fusion(f32[12,8,32,128]{3,2,1,0:T(8,128)} %get-tuple-element.149, s32[]{:T(128)S(6)} %copy.97, f32[8,8,128]{2,1,0:T(8,128)S(1)} %bitcast.156, f32[8,128]{1,0:T(8,128)} %get-tuple-element.132, f32[8,8,128]{2,1,0:T(8,128)S(1)} %bitcast.157, f32[8,8,128]{2,1,0:T(8,128)S(1)} %bitcast.158, ...), kind=kOutput, calls=%fused_computation.21.clone.1 | convolution fusion | flops 87293952 | bytes 897092 | tf_op jit(solution)/shard_map/while/body/eval_jaxpr/bmnj,bnrj->brm/dot_general | solution.py:144
  167.0 5.9 %fusion.84 = f32[12,8,32,128]{3,2,1,0:T(8,128)} fusion(f32[12,8,32,128]{3,2,1,0:T(8,128)} %get-tuple-element.149, s32[]{:T(128)S(6)} %copy.97, f32[8,8,128]{2,1,0:T(8,128)S(1)} %bitcast.156, f32[8,128]{1,0:T(8,128)} %get-tuple-element.132, f32[8,8,128]{2,1,0:T(8,128)S(1)} %bitcast.157, f32[8,8,128]{2,1,0:T(8,128)S(1)} %bitcast.158, ...), kind=kOutput, calls=%fused_computation.21.clone.1 | convolution fusion | flops 87293952 | bytes 897092 | tf_op jit(solution)/shard_map/while/body/eval_jaxpr/bmnj,bnrj->brm/dot_general | solution.py:144
  177.8 5.9 %fusion.84 = f32[12,8,32,128]{3,2,1,0:T(8,128)} fusion(f32[12,8,32,128]{3,2,1,0:T(8,128)} %get-tuple-element.149, s32[]{:T(128)S(6)} %copy.97, f32[8,8,128]{2,1,0:T(8,128)S(1)} %bitcast.156, f32[8,128]{1,0:T(8,128)} %get-tuple-element.132, f32[8,8,128]{2,1,0:T(8,128)S(1)} %bitcast.157, f32[8,8,128]{2,1,0:T(8,128)S(1)} %bitcast.158, ...), kind=kOutput, calls=%fused_computation.21.clone.1 | convolution fusion | flops 87293952 | bytes 897092 | tf_op jit(solution)/shard_map/while/body/eval_jaxpr/bmnj,bnrj->brm/dot_general | solution.py:144
  188.7 5.9 %fusion.84 = f32[12,8,32,128]{3,2,1,0:T(8,128)} fusion(f32[12,8,32,128]{3,2,1,0:T(8,128)} %get-tuple-element.149, s32[]{:T(128)S(6)} %copy.97, f32[8,8,128]{2,1,0:T(8,128)S(1)} %bitcast.156, f32[8,128]{1,0:T(8,128)} %get-tuple-element.132, f32[8,8,128]{2,1,0:T(8,128)S(1)} %bitcast.157, f32[8,8,128]{2,1,0:T(8,128)S(1)} %bitcast.158, ...), kind=kOutput, calls=%fused_computation.21.clone.1 | convolution fusion | flops 87293952 | bytes 897092 | tf_op jit(solution)/shard_map/while/body/eval_jaxpr/bmnj,bnrj->brm/dot_general | solution.py:144
  199.6 5.9 %fusion.84 = f32[12,8,32,128]{3,2,1,0:T(8,128)} fusion(f32[12,8,32,128]{3,2,1,0:T(8,128)} %get-tuple-element.149, s32[]{:T(128)S(6)} %copy.97, f32[8,8,128]{2,1,0:T(8,128)S(1)} %bitcast.156, f32[8,128]{1,0:T(8,128)} %get-tuple-element.132, f32[8,8,128]{2,1,0:T(8,128)S(1)} %bitcast.157, f32[8,8,128]{2,1,0:T(8,128)S(1)} %bitcast.158, ...), kind=kOutput, calls=%fused_computation.21.clone.1 | convolution fusion | flops 87293952 | bytes 897092 | tf_op jit(solution)/shard_map/while/body/eval_jaxpr/bmnj,bnrj->brm/dot_general | solution.py:144
  210.5 5.9 %fusion.84 = f32[12,8,32,128]{3,2,1,0:T(8,128)} fusion(f32[12,8,32,128]{3,2,1,0:T(8,128)} %get-tuple-element.149, s32[]{:T(128)S(6)} %copy.97, f32[8,8,128]{2,1,0:T(8,128)S(1)} %bitcast.156, f32[8,128]{1,0:T(8,128)} %get-tuple-element.132, f32[8,8,128]{2,1,0:T(8,128)S(1)} %bitcast.157, f32[8,8,128]{2,1,0:T(8,128)S(1)} %bitcast.158, ...), kind=kOutput, calls=%fused_computation.21.clone.1 | convolution fusion | flops 87293952 | bytes 897092 | tf_op jit(solution)/shard_map/while/body/eval_jaxpr/bmnj,bnrj->brm/dot_general | solution.py:144
  221.4 5.9 %fusion.84 = f32[12,8,32,128]{3,2,1,0:T(8,128)} fusion(f32[12,8,32,128]{3,2,1,0:T(8,128)} %get-tuple-element.149, s32[]{:T(128)S(6)} %copy.97, f32[8,8,128]{2,1,0:T(8,128)S(1)} %bitcast.156, f32[8,128]{1,0:T(8,128)} %get-tuple-element.132, f32[8,8,128]{2,1,0:T(8,128)S(1)} %bitcast.157, f32[8,8,128]{2,1,0:T(8,128)S(1)} %bitcast.158, ...), kind=kOutput, calls=%fused_computation.21.clone.1 | convolution fusion | flops 87293952 | bytes 897092 | tf_op jit(solution)/shard_map/while/body/eval_jaxpr/bmnj,bnrj->brm/dot_general | solution.py:144
  232.3 5.9 %fusion.84 = f32[12,8,32,128]{3,2,1,0:T(8,128)} fusion(f32[12,8,32,128]{3,2,1,0:T(8,128)} %get-tuple-element.149, s32[]{:T(128)S(6)} %copy.97, f32[8,8,128]{2,1,0:T(8,128)S(1)} %bitcast.156, f32[8,128]{1,0:T(8,128)} %get-tuple-element.132, f32[8,8,128]{2,1,0:T(8,128)S(1)} %bitcast.157, f32[8,8,128]{2,1,0:T(8,128)S(1)} %bitcast.158, ...), kind=kOutput, calls=%fused_computation.21.clone.1 | convolution fusion | flops 87293952 | bytes 897092 | tf_op jit(solution)/shard_map/while/body/eval_jaxpr/bmnj,bnrj->brm/dot_general | solution.py:144
  243.2 5.9 %fusion.84 = f32[12,8,32,128]{3,2,1,0:T(8,128)} fusion(f32[12,8,32,128]{3,2,1,0:T(8,128)} %get-tuple-element.149, s32[]{:T(128)S(6)} %copy.97, f32[8,8,128]{2,1,0:T(8,128)S(1)} %bitcast.156, f32[8,128]{1,0:T(8,128)} %get-tuple-element.132, f32[8,8,128]{2,1,0:T(8,128)S(1)} %bitcast.157, f32[8,8,128]{2,1,0:T(8,128)S(1)} %bitcast.158, ...), kind=kOutput, calls=%fused_computation.21.clone.1 | convolution fusion | flops 87293952 | bytes 897092 | tf_op jit(solution)/shard_map/while/body/eval_jaxpr/bmnj,bnrj->brm/dot_general | solution.py:144
  249.1 0.9 pad_maximum_fusion.3
  251.6 1.7 convolution_bitcast_fusion.3
  253.3 1.4 reshape.252
  255.4 1.2 reshape_reshape.3
  256.6 1.6 bitcast_reduce_fusion
  258.2 1.7 gather_fusion.4
  260.0 1.1 convolution_bitcast_fusion.1
  261.1 1.2 fusion.33
  262.4 2.8 fusion.37
  265.1 1.3 pad_maximum_fusion
  266.5 4.0 %gather_fusion.2 = bf16[576,2048]{1,0:T(8,128)(2,1)} fusion(bf16[288,2048]{1,0:T(8,128)(2,1)S(1)} %pad_maximum_fusion, s32[1024]{0:T(1024)S(1)} %pad_clamp_fusion.3), kind=kCustom, calls=%fused_computation.2 | custom fusion | bytes 4720896 | tf_op jit(solution)/shard_map/jit(_take)/gather | solution.py:123
  270.4 11.7 %gather.23 = bf16[96,6,64,32]{3,2,1,0:T(8,128)(2,1)} reshape(bf16[576,2048]{1,0:T(8,128)(2,1)} %gather_fusion.2) | data formatting | bytes 4718592 | tf_op jit(solution)/shard_map/jit(_take)/gather | solution.py:123
  282.1 10.3 %bitcast_add_fusion.1 = f32[96,32,128]{2,1,0:T(8,128)} fusion(f32[12,8,32,128]{3,2,1,0:T(8,128)} %get-tuple-element.37, bf16[96,64,128]{2,1,0:T(8,128)(2,1)S(1)} %copy-done, f32[32,96,64]{2,0,1:T(8,128)S(1)} %copy-done.2, bf16[96,6,64,64]{3,2,1,0:T(8,128)(2,1)} %copy.71, bf16[96,6,64,32]{3,2,1,0:T(8,128)(2,1)} %gather.23, pred[96,6]{1,0:T(8,128)(4,1)S(1)} %copy-done.7, ...), kind=kOutput, calls=%fused_computation.44 | convolution fusion | flops 204472320 | bytes 12584640 | tf_op jit(solution)/shard_map/lkr,lkm->lrm/dot_general | solution.py:134
  (188 shorter events, 69.6 us)
Async XLA Ops:
  0.0 282.1 %copy-start = (bf16[96,64,128]{2,1,0:T(8,128)(2,1)S(1)}, bf16[96,64,128]{2,1,0:T(8,128)(2,1)}, u32[]{:S(2)}) copy-start(bf16[96,64,128]{2,1,0:T(8,128)(2,1)} %param.25) | copy-start | bytes 4718596
  4.9 260.2 %collective-permute-start.1 = (bf16[96,2048]{1,0:T(8,128)(2,1)}, bf16[96,2048]{1,0:T(8,128)(2,1)}, u32[]{:S(2)}, u32[]{:S(2)}) collective-permute-start(bf16[96,2048]{1,0:T(8,128)(2,1)} %copy.66), channel_id=1, source_target_pairs={{1,0},{2,1},{3,2},{4,3},{5,4},{6,5},{7,6},{8,7},{9,8},{10,9},{11,1... | collective-permute-start | bytes 1179656 | tf_op jit(solution)/shard_map/ppermute | solution.py:36
  14.2 250.9 %collective-permute-start = (bf16[96,2048]{1,0:T(8,128)(2,1)}, bf16[96,2048]{1,0:T(8,128)(2,1)}, u32[]{:S(2)}, u32[]{:S(2)}) collective-permute-start(bf16[96,2048]{1,0:T(8,128)(2,1)} %copy.66), channel_id=1, source_target_pairs={{0,1},{1,2},{2,3},{3,4},{4,5},{5,6},{6,7},{7,8},{8,9},{9,10},{10,1... | collective-permute-start | bytes 1179656 | tf_op jit(solution)/shard_map/ppermute | solution.py:34
  16.9 97.5 %collective-permute-start.4 = (bf16[4,32,128]{2,1,0:T(8,128)(2,1)S(1)}, bf16[4,32,128]{2,1,0:T(8,128)(2,1)S(1)}, u32[]{:S(2)}, u32[]{:S(2)}) collective-permute-start(bf16[4,32,128]{2,1,0:T(8,128)(2,1)S(1)} %get-tuple-element.80), channel_id=1, source_target_pairs={{0,1},{1,2},{2,3},{3,4},{4,5},{5,6},{6,7},{7,8},{8,9},{9,10},{10,1... | collective-permute-start | bytes 98312 | tf_op jit(solution)/shard_map/ppermute | solution.py:34
  20.0 87.0 %collective-permute-start.6 = (f32[4,7,128]{2,1,0:T(8,128)S(1)}, f32[4,7,128]{2,1,0:T(8,128)S(1)}, u32[]{:S(2)}, u32[]{:S(2)}) collective-permute-start(f32[4,7,128]{2,1,0:T(8,128)S(1)} %get-tuple-element.82), channel_id=1, source_target_pairs={{0,1},{1,2},{2,3},{3,4},{4,5},{5,6},{6,7},{7,8},{8,9},{9,10},{10,1... | collective-permute-start | bytes 43016 | tf_op jit(solution)/shard_map/ppermute | solution.py:34
  22.0 13.9 %copy-start.6 = (bf16[1,64,64]{2,1,0:T(8,128)(2,1)S(1)}, bf16[1,64,64]{2,1,0:T(8,128)(2,1)}, u32[]{:S(2)}) copy-start(bf16[1,64,64]{2,1,0:T(8,128)(2,1)} %param.31) | copy-start | bytes 24580
  22.0 89.0 %collective-permute-start.7 = (f32[4,7,128]{2,1,0:T(8,128)S(1)}, f32[4,7,128]{2,1,0:T(8,128)S(1)}, u32[]{:S(2)}, u32[]{:S(2)}) collective-permute-start(f32[4,7,128]{2,1,0:T(8,128)S(1)} %get-tuple-element.83), channel_id=1, source_target_pairs={{1,0},{2,1},{3,2},{4,3},{5,4},{6,5},{7,6},{8,7},{9,8},{10,9},{11,1... | collective-permute-start | bytes 43016 | tf_op jit(solution)/shard_map/ppermute | solution.py:36
  33.8 34.7 %copy-start.11 = (s32[1,6]{1,0:T(1,128)S(1)}, s32[1,6]{1,0:T(1,128)}, u32[]{:S(2)}) copy-start(s32[1,6]{1,0:T(1,128)} %param.34) | copy-start | bytes 76
  33.9 35.4 %copy-start.12 = (s32[1,6]{1,0:T(1,128)S(1)}, s32[1,6]{1,0:T(1,128)}, u32[]{:S(2)}) copy-start(s32[1,6]{1,0:T(1,128)} %param.38) | copy-start | bytes 76
  33.9 37.1 %copy-start.8 = (s32[96,6]{0,1:T(8,128)S(1)}, s32[96,6]{0,1:T(8,128)}, u32[]{:S(2)}) copy-start(s32[96,6]{0,1:T(8,128)} %param.29) | copy-start | bytes 6916
  33.9 37.9 %copy-start.10 = (s32[96]{0:T(128)S(1)}, s32[96]{0:T(128)}, u32[]{:S(2)}) copy-start(s32[96]{0:T(128)} %param.30) | copy-start | bytes 1156
  33.9 38.5 %copy-start.9 = (s32[96,8]{0,1:T(8,128)S(1)}, s32[96,8]{0,1:T(8,128)}, u32[]{:S(2)}) copy-start(s32[96,8]{0,1:T(8,128)} %param.23) | copy-start | bytes 9220
  62.9 190.4 %all-to-all-start = ((bf16[32,2,1024]{2,1,0:T(2,128)(2,1)}), bf16[32,2,1024]{2,1,0:T(2,128)(2,1)}, u32[]{:S(2)}, u32[]{:S(2)}) async-start(bf16[32,2,1024]{2,1,0:T(2,128)(2,1)} %reshape.251), calls=%async_computation | async-start | bytes 262144 | tf_op jit(solution)/shard_map/all_to_all | solution.py:15
  107.0 10.1 %collective-permute-start.5 = (bf16[4,32,128]{2,1,0:T(8,128)(2,1)S(1)}, bf16[4,32,128]{2,1,0:T(8,128)(2,1)S(1)}, u32[]{:S(2)}, u32[]{:S(2)}) collective-permute-start(bf16[4,32,128]{2,1,0:T(8,128)(2,1)S(1)} %get-tuple-element.81), channel_id=1, source_target_pairs={{1,0},{2,1},{3,2},{4,3},{5,4},{6,5},{7,6},{8,7},{9,8},{10,9},{11,1... | collective-permute-start | bytes 98312 | tf_op jit(solution)/shard_map/ppermute | solution.py:36
  111.0 138.1 %collective-permute-start.3 = (bf16[8,2048]{1,0:T(8,128)(2,1)}, bf16[8,2048]{1,0:T(8,128)(2,1)}, u32[]{:S(2)}, u32[]{:S(2)}) collective-permute-start(bf16[8,2048]{1,0:T(8,128)(2,1)} %bitcast.123), channel_id=1, source_target_pairs={{8,0},{16,8},{24,16},{32,24},{40,32},{48,40},{56,48},{64,56},{72,6... | collective-permute-start | bytes 98312 | tf_op jit(solution)/shard_map/ppermute | solution.py:36
  114.4 134.6 %collective-permute-start.2 = (bf16[8,2048]{1,0:T(8,128)(2,1)}, bf16[8,2048]{1,0:T(8,128)(2,1)}, u32[]{:S(2)}, u32[]{:S(2)}) collective-permute-start(bf16[8,2048]{1,0:T(8,128)(2,1)} %bitcast.123), channel_id=1, source_target_pairs={{0,8},{8,16},{16,24},{24,32},{32,40},{40,48},{48,56},{56,64},{64,7... | collective-permute-start | bytes 98312 | tf_op jit(solution)/shard_map/ppermute | solution.py:34
  249.1 10.9 %copy-start.13 = (pred[6]{0:T(512)(128)(4,1)S(1)}, pred[6]{0:T(512)(128)(4,1)}, u32[]{:S(2)}) copy-start(pred[6]{0:T(512)(128)(4,1)} %compare_and_fusion.2) | copy-start | bytes 22
  249.1 13.3 %copy-start.1 = (bf16[96,64,64]{2,1,0:T(8,128)(2,1)S(1)}, bf16[96,64,64]{2,1,0:T(8,128)(2,1)}, u32[]{:S(2)}) copy-start(bf16[96,64,64]{2,1,0:T(8,128)(2,1)} %copy.78) | copy-start | bytes 2359300
  255.4 7.0 %copy-start.3 = (f32[32,64]{1,0:T(8,128)S(1)}, f32[32,64]{1,0:T(8,128)}, u32[]{:S(2)}) copy-start(f32[32,64]{1,0:T(8,128)} %convolution_bitcast_fusion.3) | copy-start | bytes 24580
  255.4 7.0 %copy-start.5 = (bf16[1,64,64]{2,1,0:T(8,128)(2,1)S(1)}, bf16[1,64,64]{2,1,0:T(8,128)(2,1)}, u32[]{:S(2)}) copy-start(bf16[1,64,64]{2,1,0:T(8,128)(2,1)} %param.32) | copy-start | bytes 24580
  270.4 11.7 %copy-start.2 = (f32[32,96,64]{2,0,1:T(8,128)S(1)}, f32[32,96,64]{2,0,1:T(8,128)}, u32[]{:S(2)}) copy-start(f32[32,96,64]{2,0,1:T(8,128)} %fusion.37) | copy-start | bytes 2359300
  270.4 11.7 %copy-start.4 = (bf16[96,6]{1,0:T(8,128)(2,1)S(1)}, bf16[96,6]{1,0:T(8,128)(2,1)}, u32[]{:S(2)}) copy-start(bf16[96,6]{1,0:T(8,128)(2,1)} %fusion.49) | copy-start | bytes 3460
  270.4 11.7 %copy-start.7 = (pred[96,6]{1,0:T(8,128)(4,1)S(1)}, pred[96,6]{1,0:T(8,128)(4,1)}, u32[]{:S(2)}) copy-start(pred[96,6]{1,0:T(8,128)(4,1)} %copy.64) | copy-start | bytes 1732
